TPU v7x, 128 devices: a whole 4x4x4 slice. The times are simulated.
128 devices in a mesh: replica: 16 (over x_lo, z, core), tensor: 8 (over y, x_hi).
Axes of the slice: x: 4 (x_hi: 2, x_lo: 2; x = x_hi * 2 + x_lo), y: 4, z: 4, core: 2. Of those that a mesh axis runs over, the one named last changes fastest.
Arguments:
- tokens: bfloat16 [8192, 1024], P('replica'), may hold values from -6 to 6
- targets: bfloat16 [8192, 1024], P('replica'), may hold values from -6 to 6
- row_ids: int32 [16, 3, 512], P('replica'), may hold values from 0 to 511
- anchor: float32 [2, 1024, 4096], P(None, None, 'tensor'), may hold values from -0.1875 to 0.1875
- momentum: float32 [16, 2, 1024, 4096], P('replica', None, None, 'tensor'), may hold values from -4 to 4
- slow: float32 [2, 1024, 4096], P(None, None, 'tensor'), may hold values from -6 to 6
Outputs:
- anchor_new: float32 [2, 1024, 4096], P(None, None, 'tensor')
- slow_new: float32 [2, 1024, 4096], P(None, None, 'tensor')
- momentum_new: float32 [16, 2, 1024, 4096], P('replica', None, None, 'tensor')
Inputs may be any that keep to these rules, and one draw needn't show every extreme that they name: `row_ids`: each id names a row within its replica's own block of 512 rows; rows may repeat.
All inputs are finite; a program needn't handle non-finite values.
Results may differ from a plain program's by a relative error of at most 0.008.
Values may be sent and summed in bfloat16 or wider, within the bound.
A program may use at most 128 MiB of HBM per device.

v0:
```python
import jax
import jax.numpy as jnp
from jax import lax
from jax.sharding import PartitionSpec as P

INNER = 3
learn_rate = 0.02
inner_beta = 0.9
slow_beta = 0.5


def passed_along(block, axis, distance):
    devices = range(lax.axis_size(axis))
    route = [((i - distance) % len(devices), i) for i in devices]
    return lax.ppermute(block, axis, route)


def gelu_pair(pre):
    coeff = 0.7978845608028654
    inner = coeff * (pre + 0.044715 * pre * pre * pre)
    tanh_val = jnp.tanh(inner)
    value = 0.5 * pre * (1.0 + tanh_val)
    slope = 0.5 * (1.0 + tanh_val) + 0.5 * pre * (1.0 - tanh_val * tanh_val) * coeff * (
        1.0 + 3.0 * 0.044715 * pre * pre
    )
    return (value, slope)


def body(tokens, targets, row_ids, anchor, momentum, slow):
    row_count = tokens.shape[0]
    scale = 1.0 / row_count
    weights = anchor
    moment = momentum[0]
    for step in range(INNER):
        if step > 0:
            incoming = passed_along(weights.astype(jnp.bfloat16), "replica", 2 ** (step - 1))
            weights = 0.5 * (weights + incoming.astype(jnp.float32))
        picks = row_ids[0, step]
        inputs = jnp.take(tokens, picks, axis=0)
        wanted = jnp.take(targets, picks, axis=0)
        weights_bf = weights.astype(jnp.bfloat16)
        pre = jnp.dot(inputs, weights_bf[0], preferred_element_type=jnp.float32)
        value, slope = gelu_pair(pre)
        hidden = value.astype(jnp.bfloat16)
        partial_out = lax.dot_general(
            hidden, weights_bf[1], (((1,), (1,)), ((), ())), preferred_element_type=jnp.float32
        )
        summed = lax.psum(partial_out, "tensor")
        error = ((summed - wanted.astype(jnp.float32)) * scale).astype(jnp.bfloat16)
        back = (jnp.dot(error, weights_bf[1], preferred_element_type=jnp.float32) * slope).astype(
            jnp.bfloat16
        )
        grad_in = lax.dot_general(
            inputs, back, (((0,), (0,)), ((), ())), preferred_element_type=jnp.float32
        )
        grad_out = lax.dot_general(
            error, hidden, (((0,), (0,)), ((), ())), preferred_element_type=jnp.float32
        )
        moment = inner_beta * moment + jnp.stack([grad_in, grad_out])
        weights = weights - learn_rate * moment
    replicas = lax.axis_size("replica")
    total = lax.psum(weights, "replica")
    mean = total / replicas
    slow_new = slow_beta * slow + (anchor - mean) / learn_rate
    anchor_new = anchor - learn_rate * slow_new
    return (anchor_new, slow_new, moment[None])


def solution(mesh):
    return jax.shard_map(
        body,
        mesh=mesh,
        in_specs=(
            P("replica", None),
            P("replica", None),
            P("replica", None, None),
            P(None, None, "tensor"),
            P("replica", None, None, "tensor"),
            P(None, None, "tensor"),
        ),
        out_specs=(
            P(None, None, "tensor"),
            P(None, None, "tensor"),
            P("replica", None, None, "tensor"),
        ),
        check_vma=False,
    )
```

profile of v0, /device:TPU:0, one launch (start us, length us, event | category | flops | bytes accessed | tf_op | source)
XLA Modules:
  0.0 625.0 jit_solution(4985330071211238763)
XLA Ops:
  7.2 0.8 fusion.103
  8.0 3.8 convert_element_type.57
  11.8 2.0 gather_fusion
  13.9 2.1 fusion.34
  16.0 1.0 copy-done.19
  17.0 2.1 fusion.56
  19.2 1.1 copy-done.2
  20.4 2.8 gather_fusion.1
  23.1 105.8 %all-reduce.5.cloned.1.call-done = f32[512,1024]{1,0:T(8,128)} async-done(((f32[512,1024]{1,0:T(8,128)}), f32[512,1024]{1,0:T(8,128)}) %all-reduce.5.cloned.1.call-update) | async-done | bytes 2097168 | tf_op jit(solution)/shard_map/psum | solution.py:48
  128.9 5.6 fusion.13
  134.5 3.5 fusion.99
  138.0 1.8 copy-done.11
  139.8 0.8 copy-done.12
  140.6 4.5 fusion.83
  145.1 2.1 gather_fusion.2
  147.2 25.8 %collective-permute-done = bf16[2,1024,512]{2,1,0:T(8,128)(2,1)} collective-permute-done((bf16[2,1024,512]{2,1,0:T(8,128)(2,1)}, bf16[2,1024,512]{2,1,0:T(8,128)(2,1)}, u32[]{:S(2)}, u32[]{:S(2)}) %collective-permute-start) | collective-permute-done | bytes 2097184 | tf_op jit(solution)/shard_map/ppermute | solution.py:15
  173.0 5.3 fusion.6
  178.3 0.8 fusion.33
  179.1 0.6 copy-done.16
  179.7 1.0 copy-done.20
  180.6 2.1 fusion.57
  182.8 0.2 all-reduce.9.cloned.1.call-start
  183.0 2.8 gather_fusion.3
  185.8 100.5 %all-reduce.7.cloned.1.call-done = f32[512,1024]{1,0:T(8,128)} async-done(((f32[512,1024]{1,0:T(8,128)}), f32[512,1024]{1,0:T(8,128)}) %all-reduce.7.cloned.1.call-update) | async-done | bytes 2097168 | tf_op jit(solution)/shard_map/psum | solution.py:48
  286.3 5.6 fusion.12
  291.9 3.5 fusion.100
  295.4 1.8 copy-done.5
  297.2 0.8 copy-done.8
  298.0 5.1 fusion.102
  303.1 1.6 collective-permute-start.1
  304.6 2.1 gather_fusion.4
  306.7 45.4 %collective-permute-done.1 = bf16[2,1024,512]{2,1,0:T(8,128)(2,1)} collective-permute-done((bf16[2,1024,512]{2,1,0:T(8,128)(2,1)}, bf16[2,1024,512]{2,1,0:T(8,128)(2,1)}, u32[]{:S(2)}, u32[]{:S(2)}) %collective-permute-start.1) | collective-permute-done | bytes 2097184 | tf_op jit(solution)/shard_map/ppermute | solution.py:15
  352.1 3.6 fusion.7
  355.7 0.8 fusion.32
  356.5 0.6 copy-done.17
  357.0 2.2 fusion.58
  359.3 0.3 all-reduce.11.cloned.1.call-start
  359.5 2.1 gather_fusion.5
  361.6 101.4 %all-reduce.9.cloned.1.call-done = f32[512,1024]{1,0:T(8,128)} async-done(((f32[512,1024]{1,0:T(8,128)}), f32[512,1024]{1,0:T(8,128)}) %all-reduce.9.cloned.1.call-update) | async-done | bytes 2097168 | tf_op jit(solution)/shard_map/psum | solution.py:48
  463.0 5.4 fusion.11
  468.4 3.4 fusion.101
  471.9 1.3 copy-done.14
  473.2 0.5 copy-done.7
  473.7 0.8 copy-done.9
  474.5 5.4 fusion.1
  479.9 7.7 %fusion.5 = f32[1,2,1024,512]{3,2,1,0:T(8,128)} fusion(f32[1,1,1024,512]{3,2,1,0:T(8,128)} %bitcast.51, f32[1,1,1024,512]{3,2,1,0:T(8,128)} %bitcast.48, f32[1,1,1024,512]{3,2,1,0:T(8,128)} %bitcast.47, f32[1,1,1024,512]{3,2,1,0:T(8,128)S(1)} %bitcast.44, f32[1,1,1024,512]{3,2,1,0:T(8,128)} %bitcast.55, f32[1,1,1024,512]{3,2,1,0:T(8,128)} %bitcast.53, ...), kind=kLoop, calls=%fused_computation.15 | loop fusion | flops 9437184 | bytes 20971520 | tf_op jit(solution)/shard_map/add | solution.py:59
  487.6 120.6 %all-reduce.11.cloned.1.call-done = f32[2,1024,512]{2,1,0:T(8,128)} async-done(((f32[2,1024,512]{2,1,0:T(8,128)}), f32[2,1024,512]{2,1,0:T(8,128)}) %all-reduce.11.cloned.1.call-update) | async-done | bytes 4194320 | tf_op jit(solution)/shard_map/psum | solution.py:62
  608.2 10.2 %multiply_subtract_fusion = (f32[2,1024,512]{2,1,0:T(8,128)}, f32[2,1024,512]{2,1,0:T(8,128)}) fusion(f32[2,1024,512]{2,1,0:T(8,128)} %param.11, f32[2,1024,512]{2,1,0:T(8,128)} %all-reduce.11.cloned.1.call-done, f32[2,1024,512]{2,1,0:T(8,128)} %param.13), kind=kLoop, calls=%fused_computation.16 | loop fusion | flops 7340032 | bytes 20971520 | tf_op jit(solution)/shard_map/sub | solution.py:65
  (48 shorter events, 0.3 us)
Async XLA Ops:
  7.2 4.7 copy-start
  7.2 121.7 %all-reduce.5.cloned.1.call-start = ((), (), s32[]{:S(2)}) async-start(), calls=%async_computation | async-start | bytes 4194304 | tf_op jit(solution)/shard_map/psum | solution.py:48
  13.9 3.1 copy-start.15
  16.0 1.0 copy-start.19
  19.1 1.2 copy-start.2
  19.2 267.1 %all-reduce.7.cloned.1.call-start = ((), (), s32[]{:S(2)}) async-start(), calls=%async_computation.1 | async-start | bytes 4194304 | tf_op jit(solution)/shard_map/psum | solution.py:48
  134.5 3.5 copy-start.3
  134.5 5.3 copy-start.11
  134.5 6.1 copy-start.12
  138.0 7.1 %copy-start.13 = (f32[1024,512]{1,0:T(8,128)}, f32[1024,512]{1,0:T(8,128)S(1)}, u32[]{:S(2)}) copy-start(f32[1024,512]{1,0:T(8,128)S(1)} %fusion.99) | copy-start | bytes 6291460
  145.1 27.9 %collective-permute-start = (bf16[2,1024,512]{2,1,0:T(8,128)(2,1)}, bf16[2,1024,512]{2,1,0:T(8,128)(2,1)}, u32[]{:S(2)}, u32[]{:S(2)}) collective-permute-start(bf16[2,1024,512]{2,1,0:T(8,128)(2,1)} %get-tuple-element.8), channel_id=1, source_target_pairs={{120,0},{0,8},{8,16},{16,24},{24,32},{32,40},{40,48},{48,56},{56,6... | collective-permute-start | bytes 6291464 | tf_op jit(solution)/shard_map/ppermute | solution.py:15
  178.3 1.4 copy-start.16
  179.7 1.0 copy-start.20
  182.8 280.2 %all-reduce.9.cloned.1.call-start = ((), (), s32[]{:S(2)}) async-start(), calls=%async_computation.2 | async-start | bytes 4194304 | tf_op jit(solution)/shard_map/psum | solution.py:48
  291.9 3.5 copy-start.4
  291.9 5.3 copy-start.5
  291.9 6.1 copy-start.8
  295.4 7.7 %copy-start.10 = (f32[1024,512]{1,0:T(8,128)}, f32[1024,512]{1,0:T(8,128)S(1)}, u32[]{:S(2)}) copy-start(f32[1024,512]{1,0:T(8,128)S(1)} %fusion.100) | copy-start | bytes 6291460
  303.1 49.0 %collective-permute-start.1 = (bf16[2,1024,512]{2,1,0:T(8,128)(2,1)}, bf16[2,1024,512]{2,1,0:T(8,128)(2,1)}, u32[]{:S(2)}, u32[]{:S(2)}) collective-permute-start(bf16[2,1024,512]{2,1,0:T(8,128)(2,1)} %get-tuple-element.6), channel_id=1, source_target_pairs={{112,0},{120,8},{0,16},{8,24},{16,32},{24,40},{32,48},{40,56},{48,... | collective-permute-start | bytes 6291464 | tf_op jit(solution)/shard_map/ppermute | solution.py:15
  355.7 1.3 copy-start.17
  357.0 2.2 copy-start.21
  359.3 249.0 %all-reduce.11.cloned.1.call-start = ((), (), s32[]{:S(2)}) async-start(), calls=%async_computation.3 | async-start | bytes 8388608 | tf_op jit(solution)/shard_map/psum | solution.py:62
  361.6 101.4 %copy-start.18 = (bf16[512,1024]{1,0:T(8,128)(2,1)}, bf16[512,1024]{1,0:T(8,128)(2,1)S(1)}, u32[]{:S(2)}) copy-start(bf16[512,1024]{1,0:T(8,128)(2,1)S(1)} %gather_fusion.5) | copy-start | bytes 3145732
  468.4 4.8 copy-start.6
  468.4 5.3 copy-start.7
  468.4 6.1 copy-start.9
  471.9 1.3 copy-start.14
  608.2 10.2 %copy-start.1 = (bf16[512,1024]{1,0:T(8,128)(2,1)S(1)}, bf16[512,1024]{1,0:T(8,128)(2,1)}, u32[]{:S(2)}) copy-start(bf16[512,1024]{1,0:T(8,128)(2,1)} %param.8) | copy-start | bytes 3145732
Sparse Core Ops, SparseCore 0:
  19.3 109.5 all-reduce.4
  182.9 103.3 all-reduce.6
  359.4 103.5 all-reduce.8
  480.1 128.1 all-reduce.10
where the time goes:
time: 625 us
  waiting for transfers between devices  500 us (80%)
  other arithmetic  45.6 us (7%)
  matrix products  37 us (6%)
  local copies, waits for them, and re-layouts  26.7 us (4%)
  between operations  14 us (2%)
    psum x3, waiting for transfers between devices, body(): summed = lax.psum(partial_out, 'tensor')  308 us
    psum x1, waiting for transfers between devices, body(): total = lax.psum(weights, 'replica')  121 us
    ppermute x2, waiting for transfers between devices, passed_along(): return lax.ppermute(block, axis, route)  71.2 us
    dot_general x3, matrix products, body(): lax.dot_general(inputs, back, (((0,), (0,)), ((), ())), preferred_element...  16.6 us
    convert_element_type x3, other arithmetic, body(): weights_bf = weights.astype(jnp.bfloat16)  12.7 us
  transfers between devices with their start and end apart: 6, of which 6 were waited for; matrix products, arithmetic and copies ran while one was open for 3% of the time, Pallas kernels for 0%

commit v1 on v0

--- a/solution.py
+++ b/solution.py
@@ -59,7 +59,7 @@
         moment = inner_beta * moment + jnp.stack([grad_in, grad_out])
         weights = weights - learn_rate * moment
     replicas = lax.axis_size("replica")
-    total = lax.psum(weights, "replica")
+    total = jnp.sum(lax.all_gather(weights, "replica"), axis=0)
     mean = total / replicas
     slow_new = slow_beta * slow + (anchor - mean) / learn_rate
     anchor_new = anchor - learn_rate * slow_new

time: 625 us -> 849 us (1.36)
  waiting for transfers between devices: 500 us -> 698 us
  other arithmetic: 45.6 us -> 68.8 us
    all_gather x0 -> x1, waiting for transfers between devices: none -> 320 us  [body(): total = jnp.sum(lax.all_gather(weights, 'replica'), axis=0)]
    psum x1 -> x0, waiting for transfers between devices: 121 us -> none  [body(): total = lax.psum(weights, 'replica')]
    reduce_sum x0 -> x1, other arithmetic: none -> 23.2 us  [body(): total = jnp.sum(lax.all_gather(weights, 'replica'), axis=0)]
  transfers between devices with their start and end apart: 6 -> 6, of which waited for: 6 -> 6; matrix products, arithmetic and copies ran while one was open for 3% -> 2% of each run, Pallas kernels for 0% -> 0%
where the time goes in v1:
time: 849 us; the launch traced here: 847 us
  waiting for transfers between devices  698 us (82%)
  other arithmetic  68.8 us (8%)
  matrix products  37 us (4%)
  local copies, waits for them, and re-layouts  26.9 us (3%)
  between operations  14 us (2%)
    all_gather x1, waiting for transfers between devices, body(): total = jnp.sum(lax.all_gather(weights, 'replica'), axis=0)  320 us
    psum x3, waiting for transfers between devices, body(): summed = lax.psum(partial_out, 'tensor')  308 us
    ppermute x2, waiting for transfers between devices, passed_along(): return lax.ppermute(block, axis, route)  71.1 us
    reduce_sum x1, other arithmetic, body(): total = jnp.sum(lax.all_gather(weights, 'replica'), axis=0)  23.2 us
  transfers between devices with their start and end apart: 6, of which 6 were waited for; matrix products, arithmetic and copies ran while one was open for 2% of the time, Pallas kernels for 0%

profile of v1, /device:TPU:0, one launch (start us, length us, event | category | flops | bytes accessed | tf_op | source)
XLA Modules:
  0.0 847.2 jit_solution(18049190229910486934)
XLA Ops:
  7.2 0.8 fusion.103
  8.1 3.8 convert_element_type.57
  11.8 2.0 gather_fusion
  13.9 2.1 fusion.34
  16.0 1.0 copy-done.19
  17.0 2.1 fusion.56
  19.2 1.1 copy-done.2
  20.4 2.8 gather_fusion.1
  23.1 105.8 %all-reduce.4.cloned.1.call-done = f32[512,1024]{1,0:T(8,128)} async-done(((f32[512,1024]{1,0:T(8,128)}), f32[512,1024]{1,0:T(8,128)}) %all-reduce.4.cloned.1.call-update) | async-done | bytes 2097168 | tf_op jit(solution)/shard_map/psum | solution.py:48
  128.9 5.6 fusion.13
  134.5 3.5 fusion.99
  138.0 1.8 copy-done.11
  139.8 0.8 copy-done.12
  140.6 4.5 fusion.83
  145.1 2.1 gather_fusion.2
  147.1 25.8 %collective-permute-done = bf16[2,1024,512]{2,1,0:T(8,128)(2,1)} collective-permute-done((bf16[2,1024,512]{2,1,0:T(8,128)(2,1)}, bf16[2,1024,512]{2,1,0:T(8,128)(2,1)}, u32[]{:S(2)}, u32[]{:S(2)}) %collective-permute-start) | collective-permute-done | bytes 2097184 | tf_op jit(solution)/shard_map/ppermute | solution.py:15
  172.9 5.3 fusion.6
  178.3 0.8 fusion.33
  179.0 0.6 copy-done.16
  179.7 1.1 copy-done.20
  180.7 2.1 fusion.57
  183.1 2.8 gather_fusion.3
  185.9 100.6 %all-reduce.6.cloned.1.call-done = f32[512,1024]{1,0:T(8,128)} async-done(((f32[512,1024]{1,0:T(8,128)}), f32[512,1024]{1,0:T(8,128)}) %all-reduce.6.cloned.1.call-update) | async-done | bytes 2097168 | tf_op jit(solution)/shard_map/psum | solution.py:48
  286.4 5.6 fusion.12
  292.1 3.5 fusion.100
  295.6 1.8 copy-done.5
  297.4 0.8 copy-done.8
  298.2 5.1 fusion.102
  303.3 1.6 collective-permute-start.1
  304.8 2.1 gather_fusion.4
  306.9 45.4 %collective-permute-done.1 = bf16[2,1024,512]{2,1,0:T(8,128)(2,1)} collective-permute-done((bf16[2,1024,512]{2,1,0:T(8,128)(2,1)}, bf16[2,1024,512]{2,1,0:T(8,128)(2,1)}, u32[]{:S(2)}, u32[]{:S(2)}) %collective-permute-start.1) | collective-permute-done | bytes 2097184 | tf_op jit(solution)/shard_map/ppermute | solution.py:15
  352.3 3.6 fusion.7
  355.9 0.8 fusion.32
  356.6 0.6 copy-done.17
  357.2 2.2 fusion.58
  359.4 0.3 all-gather.3.cloned.1.call-start
  359.7 2.1 gather_fusion.5
  361.8 101.4 %all-reduce.8.cloned.1.call-done = f32[512,1024]{1,0:T(8,128)} async-done(((f32[512,1024]{1,0:T(8,128)}), f32[512,1024]{1,0:T(8,128)}) %all-reduce.8.cloned.1.call-update) | async-done | bytes 2097168 | tf_op jit(solution)/shard_map/psum | solution.py:48
  463.2 5.3 fusion.11
  468.5 3.4 fusion.101
  472.0 1.3 copy-done.14
  473.3 0.5 copy-done.7
  473.8 0.8 copy-done.9
  474.6 5.4 fusion.1
  480.1 7.7 fusion.5
  487.7 319.5 %all-gather.3.cloned.1.call-done = f32[32,1024,512]{2,1,0:T(8,128)} async-done(((f32[2,1024,512]{2,1,0:T(8,128)}), f32[32,1024,512]{2,1,0:T(8,128)}) %all-gather.3.cloned.1.call-update) | async-done | bytes 67108880 | tf_op jit(solution)/shard_map/all_gather | solution.py:62
  807.3 23.2 %reduce_sum.9 = f32[2,1024,512]{2,1,0:T(8,128)} reduce(f32[16,2,1024,512]{3,2,1,0:T(8,128)} %bitcast.16, f32[]{:T(128)} %constant.14.clone.1), dimensions={0}, to_apply=%region_3.5 | reduce | flops 15728640 | bytes 71303168 | tf_op jit(solution)/shard_map/reduce_sum | solution.py:62
  830.4 10.2 %multiply_subtract_fusion = (f32[2,1024,512]{2,1,0:T(8,128)}, f32[2,1024,512]{2,1,0:T(8,128)}) fusion(f32[2,1024,512]{2,1,0:T(8,128)} %param.11, f32[2,1024,512]{2,1,0:T(8,128)} %reduce_sum.9, f32[2,1024,512]{2,1,0:T(8,128)} %param.13), kind=kLoop, calls=%fused_computation.16 | loop fusion | flops 7340032 | bytes 20971520 | tf_op jit(solution)/shard_map/sub | solution.py:65
  (49 shorter events, 0.5 us)
Async XLA Ops:
  7.2 4.7 copy-start
  7.2 121.7 %all-reduce.4.cloned.1.call-start = ((), (), s32[]{:S(2)}) async-start(), calls=%async_computation | async-start | bytes 4194304 | tf_op jit(solution)/shard_map/psum | solution.py:48
  13.9 3.1 copy-start.15
  16.0 1.0 copy-start.19
  19.1 1.2 copy-start.2
  19.2 267.3 %all-reduce.6.cloned.1.call-start = ((), (), s32[]{:S(2)}) async-start(), calls=%async_computation.1 | async-start | bytes 4194304 | tf_op jit(solution)/shard_map/psum | solution.py:48
  134.5 3.5 copy-start.3
  134.5 5.3 copy-start.11
  134.5 6.1 copy-start.12
  138.0 7.1 copy-start.13
  145.0 27.9 %collective-permute-start = (bf16[2,1024,512]{2,1,0:T(8,128)(2,1)}, bf16[2,1024,512]{2,1,0:T(8,128)(2,1)}, u32[]{:S(2)}, u32[]{:S(2)}) collective-permute-start(bf16[2,1024,512]{2,1,0:T(8,128)(2,1)} %get-tuple-element.8), channel_id=1, source_target_pairs={{120,0},{0,8},{8,16},{16,24},{24,32},{32,40},{40,48},{48,56},{56,6... | collective-permute-start | bytes 6291464 | tf_op jit(solution)/shard_map/ppermute | solution.py:15
  178.3 1.4 copy-start.16
  179.7 1.1 copy-start.20
  182.9 280.3 %all-reduce.8.cloned.1.call-start = ((), (), s32[]{:S(2)}) async-start(), calls=%async_computation.2 | async-start | bytes 4194304 | tf_op jit(solution)/shard_map/psum | solution.py:48
  292.1 3.5 copy-start.4
  292.1 5.3 copy-start.5
  292.1 6.1 copy-start.8
  295.6 7.7 copy-start.10
  303.3 49.0 %collective-permute-start.1 = (bf16[2,1024,512]{2,1,0:T(8,128)(2,1)}, bf16[2,1024,512]{2,1,0:T(8,128)(2,1)}, u32[]{:S(2)}, u32[]{:S(2)}) collective-permute-start(bf16[2,1024,512]{2,1,0:T(8,128)(2,1)} %get-tuple-element.6), channel_id=1, source_target_pairs={{112,0},{120,8},{0,16},{8,24},{16,32},{24,40},{32,48},{40,56},{48,... | collective-permute-start | bytes 6291464 | tf_op jit(solution)/shard_map/ppermute | solution.py:15
  355.8 1.4 copy-start.17
  357.2 2.2 copy-start.21
  359.4 447.9 %all-gather.3.cloned.1.call-start = ((), (), s32[]{:S(2)}) async-start(), calls=%async_computation.3 | async-start | bytes 71303168 | tf_op jit(solution)/shard_map/all_gather | solution.py:62
  361.8 101.4 %copy-start.18 = (bf16[512,1024]{1,0:T(8,128)(2,1)}, bf16[512,1024]{1,0:T(8,128)(2,1)S(1)}, u32[]{:S(2)}) copy-start(bf16[512,1024]{1,0:T(8,128)(2,1)S(1)} %gather_fusion.5) | copy-start | bytes 3145732
  468.5 4.8 copy-start.6
  468.5 5.3 copy-start.7
  468.5 6.1 copy-start.9
  472.0 1.4 copy-start.14
  830.4 10.2 %copy-start.1 = (bf16[512,1024]{1,0:T(8,128)(2,1)S(1)}, bf16[512,1024]{1,0:T(8,128)(2,1)}, u32[]{:S(2)}) copy-start(bf16[512,1024]{1,0:T(8,128)(2,1)} %param.8) | copy-start | bytes 3145732
Sparse Core Ops, SparseCore 0:
  19.3 109.5 all-reduce.3
  183.0 103.4 all-reduce.5
  359.5 103.6 all-reduce.7
  480.2 327.0 all-gather.2
